TPU v7x, 256 devices: a whole 4x4x8 slice. The times are simulated.
256 devices in a mesh: trial: 8 (over y_hi, x), dp: 8 (over z), tensor: 4 (over y_lo, core).
Axes of the slice: x: 4, y: 4 (y_hi: 2, y_lo: 2; y = y_hi * 2 + y_lo), z: 8, core: 2. Of those that a mesh axis runs over, the one named last changes fastest.
Arguments:
- residual_rows: bfloat16 [32768, 8192], P(('trial', 'dp', 'tensor'))
- input_norm_weight: float32 [8192], replicated, may hold values from 0.25 to 1.75
- trial_row_index: int32 [8, 4096], P(None, 'dp'), may hold values from 0 to 127, as said below
- keyvalue_weight: bfloat16 [8192, 2048], P('tensor'), may hold values from -0.0625 to 0.0625
- adapter_down_weight: bfloat16 [8, 8192, 128], P('trial', 'tensor'), may hold values from -0.0625 to 0.0625
- adapter_up_weight: bfloat16 [8, 64, 2048], P('trial'), may hold values from -0.75 to 0.75
- keyvalue_gradient: bfloat16 [8, 4096, 2048], P('trial', ('dp', 'tensor')), may hold values from -6 to 6
Outputs:
- keyvalue_output: float32 [8, 4096, 2048], P('trial', ('dp', 'tensor'))
- grad_a: float32 [8, 128, 8192], P('trial', 'dp', 'tensor')
- grad_b: float32 [8, 64, 2048], P('trial', None, ('dp', 'tensor'))
Inputs may be any that keep to these rules, and one draw needn't show every extreme that they name: `trial_row_index`: within each trial, each index of dp and each block of 16 consecutive tokens taken from one source device, the rows named are distinct.
All inputs are finite; a program needn't handle non-finite values.
Results may differ from a plain program's by a relative error of at most 0.0041.
Values may be sent and summed in bfloat16 or wider, within the bound.
A program may use at most 64 MiB of HBM per device.

v0:
```python
import jax
import jax.numpy as jnp
from jax import lax
from jax.sharding import PartitionSpec as P

adapter_scale = 2.0
norm_eps = 1e-05


def shards(
    residual_rows,
    input_norm_weight,
    trial_row_index,
    keyvalue_weight,
    adapter_down_weight,
    adapter_up_weight,
    keyvalue_gradient,
):
    trials = lax.axis_size("trial")
    tensors = lax.axis_size("tensor")
    dps = lax.axis_size("dp")
    tok_dev = trial_row_index.shape[1]
    select = tok_dev // (trials * tensors)
    normed_input = keyvalue_weight.shape[0]
    kv_width = keyvalue_weight.shape[1]
    keyvalue_half = kv_width // 2
    rank_index = adapter_up_weight.shape[1]
    pool_dev = residual_rows.shape[0]
    highest_precision = lax.Precision.HIGHEST
    source = lax.axis_index("trial") * tensors + lax.axis_index("tensor")
    picks = lax.dynamic_slice_in_dim(trial_row_index, source * select, select, 1).reshape(-1)
    onehot = (picks[:, None] == jnp.arange(pool_dev, dtype=jnp.int32)[None, :]).astype(jnp.bfloat16)
    wide = jnp.dot(onehot, residual_rows, preferred_element_type=jnp.float32)
    msq = jnp.mean(wide * wide, axis=1, keepdims=True)
    chosen = (wide * lax.rsqrt(msq + norm_eps) * input_norm_weight[None, :]).astype(jnp.bfloat16)
    chosen = chosen.reshape(trials, select, tensors, normed_input).transpose(0, 2, 1, 3)
    arrived = lax.all_to_all(
        chosen.reshape(trials * tensors, select, normed_input),
        ("trial", "tensor"),
        split_axis=0,
        concat_axis=0,
        tiled=True,
    )
    rows = arrived.reshape(tok_dev, normed_input)
    up_weight = adapter_up_weight[0].astype(jnp.float32)
    grad_in = keyvalue_gradient[0].astype(jnp.float32)
    key_gradient_full = jnp.dot(
        grad_in[:, :keyvalue_half], up_weight[:, :keyvalue_half].T, precision=highest_precision
    )
    value_gradient_full = jnp.dot(
        grad_in[:, keyvalue_half:], up_weight[:, keyvalue_half:].T, precision=highest_precision
    )
    rank_gradient = (
        adapter_scale * jnp.concatenate([key_gradient_full, value_gradient_full], axis=1)
    ).astype(jnp.bfloat16)
    every_rank = lax.all_gather(rank_gradient, "tensor", axis=0, tiled=True)
    grad_a_term = lax.dot_general(
        every_rank, rows, (((0,), (0,)), ((), ())), preferred_element_type=jnp.float32
    )
    down_weight = adapter_down_weight[0]
    keyval = jnp.dot(rows, keyvalue_weight, preferred_element_type=jnp.float32)
    ranks = jnp.dot(rows, down_weight, preferred_element_type=jnp.float32)
    summed = lax.psum_scatter(
        jnp.concatenate([keyval, ranks], axis=1), "tensor", scatter_dimension=0, tiled=True
    )
    frozen_output_local = summed[:, :kv_width]
    local_rank_rows = summed[:, kv_width:]
    adapter_key = jnp.dot(
        local_rank_rows[:, :rank_index], up_weight[:, :keyvalue_half], precision=highest_precision
    )
    adapter_value = jnp.dot(
        local_rank_rows[:, rank_index:], up_weight[:, keyvalue_half:], precision=highest_precision
    )
    keyvalue_output = frozen_output_local + adapter_scale * jnp.concatenate(
        [adapter_key, adapter_value], axis=1
    )
    grad_a = lax.psum_scatter(grad_a_term, "dp", scatter_dimension=0, tiled=True)
    key_down_gradient = jnp.dot(
        local_rank_rows[:, :rank_index].T, grad_in[:, :keyvalue_half], precision=highest_precision
    )
    value_down_gradient = jnp.dot(
        local_rank_rows[:, rank_index:].T, grad_in[:, keyvalue_half:], precision=highest_precision
    )
    up_gradient_term = adapter_scale * jnp.concatenate(
        [key_down_gradient, value_down_gradient], axis=1
    )
    width = up_gradient_term.shape[1] // (dps * tensors)
    up_gradient_term = (
        up_gradient_term.reshape(rank_index, dps, tensors, width)
        .transpose(0, 2, 1, 3)
        .reshape(rank_index, dps * tensors * width)
    )
    grad_b = lax.psum_scatter(up_gradient_term, "tensor", scatter_dimension=1, tiled=True)
    grad_b = lax.psum_scatter(grad_b, "dp", scatter_dimension=1, tiled=True)
    return (keyvalue_output[None], grad_a[None], grad_b[None])


def solution(mesh):
    return jax.shard_map(
        shards,
        mesh=mesh,
        in_specs=(
            P(("trial", "dp", "tensor"), None),
            P(),
            P(None, "dp"),
            P("tensor", None),
            P("trial", "tensor", None),
            P("trial", None, None),
            P("trial", ("dp", "tensor"), None),
        ),
        out_specs=(
            P("trial", ("dp", "tensor"), None),
            P("trial", "dp", "tensor"),
            P("trial", None, ("dp", "tensor")),
        ),
        check_vma=False,
    )
```

profile of v0, /device:TPU:4, one launch (start us, length us, event | category | flops | bytes accessed | tf_op | source)
XLA Modules:
  0.0 229.4 jit_solution(2438023686047598556)
XLA Ops:
  7.2 0.0 copy-start
  7.2 0.0 reduce-scatter.7.cloned.1.call-start
  7.2 0.9 constant_dynamic-slice_fusion
  8.1 0.1 eq.15
  8.2 0.6 copy-done
  8.8 0.8 multiply_reduce_fusion
  9.6 0.0 copy-done.6
  9.6 1.8 multiply_convert_fusion
  11.5 4.5 %reshape.31 = bf16[8,16,4,2048]{3,2,1,0:T(4,128)(2,1)} reshape(bf16[128,8192]{1,0:T(8,128)(2,1)} %multiply_convert_fusion) | data formatting | bytes 4194304 | tf_op jit(solution)/shard_map/reshape | solution.py:36
  16.0 2.8 %copy.15 = bf16[8,16,4,2048]{3,1,2,0:T(8,128)(2,1)S(1)} copy(bf16[8,16,4,2048]{3,2,1,0:T(4,128)(2,1)} %reshape.31) | data formatting | bytes 4194304 | tf_op jit(solution)/shard_map/reshape | solution.py:36
  18.7 0.0 copy-start.4
  18.8 34.8 %all_to_all.5 = bf16[32,16,2048]{2,1,0:T(8,128)(2,1)S(1)} all-to-all(bf16[32,16,2048]{2,1,0:T(8,128)(2,1)S(1)} %bitcast.28), channel_id=1, replica_groups=mesh['trial'=8,'dp'=8,'tensor'=4] {'trial','tensor'}, dimensions={0} | all-to-all | bytes 4194304 | tf_op jit(solution)/shard_map/all_to_all | solution.py:37
  53.6 0.0 copy-done.4
  53.6 0.7 fusion.2
  54.3 0.6 copy-done.1
  54.9 6.9 %fusion.25 = f32[512,2048]{1,0:T(8,128)S(1)} fusion(bf16[512,2048]{1,0:T(8,128)(2,1)S(1)} %bitcast.26, bf16[2048,2048]{1,0:T(8,128)(2,1)} %param.10), kind=kOutput, calls=%fused_computation.35 | convolution fusion | flops 4294967296 | bytes 14680064 | tf_op jit(solution)/shard_map/dot_general | solution.py:61
  61.8 2.4 %pad_maximum_fusion = f32[512,2176]{1,0:T(8,128)} fusion(f32[512,128]{1,0:T(8,128)S(1)} %fusion.2, f32[512,2048]{1,0:T(8,128)S(1)} %fusion.25), kind=kLoop, calls=%fused_computation | loop fusion | flops 1114112 | bytes 8912896 | tf_op jit(solution)/shard_map/concatenate | solution.py:64
  64.2 0.0 reduce-scatter.7.cloned.1.call-update
  64.2 0.0 reduce-scatter.11.cloned.1.call-start
  64.3 51.0 %reduce-scatter.7.cloned.1.call-done = f32[128,2176]{1,0:T(8,128)} async-done(((f32[512,2176]{1,0:T(8,128)}), f32[128,2176]{1,0:T(8,128)}) %reduce-scatter.7.cloned.1.call-update) | async-done | bytes 1114128 | tf_op jit(solution)/shard_map/reduce_scatter | solution.py:63
  115.3 0.0 copy-done.3
  115.3 1.2 fusion.8
  116.5 0.3 concatenate.20
  116.8 1.4 fusion.4
  118.2 0.3 concatenate.21
  118.6 0.3 fusion.1
  118.9 0.0 copy-start.5
  118.9 0.1 copy.17
  119.0 1.2 reshape.34
  120.1 0.0 reduce-scatter.11.cloned.1.call-update
  120.2 0.0 reduce-scatter.13.cloned.1.call-start
  120.2 0.0 copy-done.5
  120.2 1.2 fusion.10
  121.4 1.2 fusion.6
  122.6 5.4 %all_gather.3 = bf16[512,128]{0,1:T(8,128)(2,1)S(1)} all-gather(bf16[128,128]{0,1:T(8,128)(2,1)S(1)} %fusion.18), channel_id=1, replica_groups=mesh['trial'=8,'dp'=8,'tensor'=4] {'tensor'}, dimensions={0}, use_global_device_ids=true | all-gather | bytes 163840 | tf_op jit(solution)/shard_map/all_gather | solution.py:56
  128.0 14.0 %reduce-scatter.11.cloned.1.call-done = f32[64,512]{1,0:T(8,128)} async-done(((f32[64,2048]{1,0:T(8,128)}), f32[64,512]{1,0:T(8,128)}) %reduce-scatter.11.cloned.1.call-update) | async-done | bytes 131088 | tf_op jit(solution)/shard_map/reduce_scatter | solution.py:93
  142.0 1.7 copy.19
  143.7 0.0 reduce-scatter.13.cloned.1.call-update
  143.8 0.0 copy-start.2
  143.8 0.0 reduce-scatter.9.cloned.1.call-start
  143.8 3.1 %fusion.26 = f32[128,2048]{1,0:T(8,128)} fusion(bf16[512,128]{0,1:T(8,128)(2,1)S(1)} %all_gather.3, bf16[512,2048]{1,0:T(8,128)(2,1)} %bitcast.27), kind=kOutput, calls=%fused_computation.36 | convolution fusion | flops 268435456 | bytes 3276800 | tf_op jit(solution)/shard_map/dot_general | solution.py:57
  146.9 0.0 reduce-scatter.9.cloned.1.call-update
  146.9 1.3 fusion.13
  148.3 1.3 fusion.16
  149.5 1.1 fusion
  150.7 31.6 %reduce-scatter.13.cloned.1.call-done = f32[64,64]{1,0:T(8,128)} async-done(((f32[512,64]{1,0:T(8,128)}), f32[64,64]{1,0:T(8,128)}) %reduce-scatter.13.cloned.1.call-update) | async-done | bytes 16400
  182.3 1.5 copy.20
  183.8 39.1 %reduce-scatter.9.cloned.1.call-done = f32[16,2048]{1,0:T(8,128)} async-done(((f32[128,2048]{1,0:T(8,128)}), f32[16,2048]{1,0:T(8,128)}) %reduce-scatter.9.cloned.1.call-update) | async-done | bytes 131088 | tf_op jit(solution)/shard_map/reduce_scatter | solution.py:77
  (6 shorter events, 0.0 us)
Async XLA Ops:
  7.2 1.6 copy-start
  7.2 108.1 %reduce-scatter.7.cloned.1.call-start = ((), (), s32[]{:S(2)}) async-start(), calls=%async_computation.5 | async-start | bytes 5570560 | tf_op jit(solution)/shard_map/reduce_scatter | solution.py:63
  8.8 0.8 copy-start.6
  18.7 34.8 %copy-start.4 = (bf16[1,2048,128]{2,1,0:T(8,128)(2,1)S(1)}, bf16[1,2048,128]{2,1,0:T(8,128)(2,1)}, u32[]{:S(2)}) copy-start(bf16[1,2048,128]{2,1,0:T(8,128)(2,1)} %param.11) | copy-start | bytes 1572868
  53.6 1.3 copy-start.1
  64.2 51.1 %copy-start.3 = (bf16[1,128,2048]{2,1,0:T(8,128)(2,1)S(1)}, bf16[1,128,2048]{2,1,0:T(8,128)(2,1)}, u32[]{:S(2)}) copy-start(bf16[1,128,2048]{2,1,0:T(8,128)(2,1)} %param.13) | copy-start | bytes 1572868
  64.2 77.8 %reduce-scatter.11.cloned.1.call-start = ((), (), s32[]{:S(2)}) async-start(), calls=%async_computation.7 | async-start | bytes 655360 | tf_op jit(solution)/shard_map/reduce_scatter | solution.py:93
  118.9 1.3 copy-start.5
  120.2 62.1 %reduce-scatter.13.cloned.1.call-start = ((), (), s32[]{:S(2)}) async-start(), calls=%async_computation.8 | async-start | bytes 294912
  143.8 3.2 %copy-start.2 = (f32[128,2176]{1,0:T(8,128)S(1)}, f32[128,2176]{1,0:T(8,128)}, u32[]{:S(2)}) copy-start(f32[128,2176]{1,0:T(8,128)} %reduce-scatter.7.cloned.1.call-done) | copy-start | bytes 3342340
  143.8 79.1 %reduce-scatter.9.cloned.1.call-start = ((), (), s32[]{:S(2)}) async-start(), calls=%async_computation.6 | async-start | bytes 1179648 | tf_op jit(solution)/shard_map/reduce_scatter | solution.py:77
Sparse Core Ops, SparseCore 0:
  64.3 50.9 reduce-scatter.6
  120.3 21.6 reduce-scatter.10
  144.5 37.7 reduce-scatter.12
  185.4 37.3 reduce-scatter.8
where the time goes:
time: 230 us; the launch traced here: 229 us
  waiting for transfers between devices  136 us (59%)
  blocking collectives  40.3 us (18%)
  matrix products  18.9 us (8%)
  local copies, waits for them, and re-layouts  14.6 us (6%)
  between operations  13.9 us (6%)
  other arithmetic  5.7 us (2%)
    reduce_scatter x1, waiting for transfers between devices, shards(): lax.psum_scatter(jnp.concatenate([keyval, ranks], axis=1), 'tensor', scat...  51 us
    reduce_scatter x1, waiting for transfers between devices, shards(): lax.psum_scatter(grad_a_term, 'dp', scatter_dimension=0, tiled=True)  39.1 us
    all_to_all x1, blocking collectives, shards(): lax.all_to_all(chosen.reshape(trials * tensors, select, normed_input), ('...  34.8 us
    unnamed x5, waiting for transfers between devices  31.7 us
    reduce_scatter x1, waiting for transfers between devices, shards(): lax.psum_scatter(up_gradient_term, 'tensor', scatter_dimension=1, tiled=T...  14 us
    reshape x2, local copies, waits for them, and re-layouts, shards(): chosen.reshape(trials, select, tensors, normed_input).transpose(0, 2, 1, 3)  7.26 us
    dot_general x1, matrix products, shards(): keyval = jnp.dot(rows, keyvalue_weight, preferred_element_type=jnp.float32)  6.88 us
    all_gather x1, blocking collectives, shards(): every_rank = lax.all_gather(rank_gradient, 'tensor', axis=0, tiled=True)  5.45 us
  transfers between devices with their start and end apart: 4, of which 4 were waited for; matrix products, arithmetic and copies ran while one was open for 5% of the time, Pallas kernels for 0%

commit v1 on v0

--- a/solution.py
+++ b/solution.py
@@ -53,7 +53,9 @@
     rank_gradient = (
         adapter_scale * jnp.concatenate([key_gradient_full, value_gradient_full], axis=1)
     ).astype(jnp.bfloat16)
-    every_rank = lax.all_gather(rank_gradient, "tensor", axis=0, tiled=True)
+    every_rank = jnp.concatenate(
+        lax.all_to_all(jnp.stack([rank_gradient] * lax.axis_size("tensor")), "tensor", 0, 0), axis=0
+    )
     grad_a_term = lax.dot_general(
         every_rank, rows, (((0,), (0,)), ((), ())), preferred_element_type=jnp.float32
     )

time: 230 us -> 230 us (level)
  blocking collectives: 40.3 us -> 34.8 us
  starting transfers between devices: 0.16 us -> 3.49 us
    all_gather x1 -> x0, blocking collectives: 5.45 us -> none  [shards(): every_rank = lax.all_gather(rank_gradient, 'tensor', axis=0, tiled=True)]
    all_to_all x0 -> x1, starting transfers between devices: none -> 3.33 us  [shards(): lax.all_to_all(jnp.stack([rank_gradient] * lax.axis_size('tensor')), 'ten...]
  transfers between devices with their start and end apart: 4 -> 5, of which waited for: 4 -> 4; matrix products, arithmetic and copies ran while one was open for 5% -> 6% of each run, Pallas kernels for 0% -> 0%
where the time goes in v1:
time: 230 us; the launch traced here: 229 us
  waiting for transfers between devices  137 us (60%)
  blocking collectives  34.8 us (15%)
  matrix products  19 us (8%)
  local copies, waits for them, and re-layouts  15.3 us (7%)
  between operations  14 us (6%)
  other arithmetic  5.7 us (2%)
  starting transfers between devices  3.49 us (2%)
    reduce_scatter x1, waiting for transfers between devices, shards(): lax.psum_scatter(jnp.concatenate([keyval, ranks], axis=1), 'tensor', scat...  51 us
    reduce_scatter x1, waiting for transfers between devices, shards(): lax.psum_scatter(grad_a_term, 'dp', scatter_dimension=0, tiled=True)  39.1 us
    all_to_all x1, blocking collectives, shards(): lax.all_to_all(chosen.reshape(trials * tensors, select, normed_input), ('...  34.8 us
    unnamed x5, waiting for transfers between devices  31.9 us
    reduce_scatter x1, waiting for transfers between devices, shards(): lax.psum_scatter(up_gradient_term, 'tensor', scatter_dimension=1, tiled=T...  15 us
    reshape x2, local copies, waits for them, and re-layouts, shards(): chosen.reshape(trials, select, tensors, normed_input).transpose(0, 2, 1, 3)  7.25 us
    dot_general x1, matrix products, shards(): keyval = jnp.dot(rows, keyvalue_weight, preferred_element_type=jnp.float32)  6.88 us
  transfers between devices with their start and end apart: 5, of which 4 were waited for; matrix products, arithmetic and copies ran while one was open for 6% of the time, Pallas kernels for 0%

profile of v1, /device:TPU:4, one launch (start us, length us, event | category | flops | bytes accessed | tf_op | source)
XLA Modules:
  0.0 229.4 jit_solution(10652704652752377426)
XLA Ops:
  7.2 0.0 copy-start
  7.2 0.0 reduce-scatter.7.cloned.1.call-start
  7.2 0.9 constant_dynamic-slice_fusion
  8.1 0.1 eq.15
  8.2 0.6 copy-done
  8.8 0.8 multiply_reduce_fusion
  9.6 1.9 multiply_convert_fusion
  11.5 4.5 %reshape.41 = bf16[8,16,4,2048]{3,2,1,0:T(4,128)(2,1)} reshape(bf16[128,8192]{1,0:T(8,128)(2,1)} %multiply_convert_fusion) | data formatting | bytes 4194304 | tf_op jit(solution)/shard_map/reshape | solution.py:36
  16.0 2.8 %copy.17 = bf16[8,16,4,2048]{3,1,2,0:T(8,128)(2,1)S(1)} copy(bf16[8,16,4,2048]{3,2,1,0:T(4,128)(2,1)} %reshape.41) | data formatting | bytes 4194304 | tf_op jit(solution)/shard_map/reshape | solution.py:36
  18.7 0.0 copy-start.4
  18.8 34.8 %all_to_all.10 = bf16[32,16,2048]{2,1,0:T(8,128)(2,1)S(1)} all-to-all(bf16[32,16,2048]{2,1,0:T(8,128)(2,1)S(1)} %bitcast.29), channel_id=1, replica_groups=mesh['trial'=8,'dp'=8,'tensor'=4] {'trial','tensor'}, dimensions={0} | all-to-all | bytes 4194304 | tf_op jit(solution)/shard_map/all_to_all | solution.py:37
  53.6 0.0 copy-done.4
  53.6 0.7 fusion.2
  54.3 0.6 copy-done.1
  54.9 6.9 %fusion.25 = f32[512,2048]{1,0:T(8,128)S(1)} fusion(bf16[512,2048]{1,0:T(8,128)(2,1)S(1)} %bitcast.27, bf16[2048,2048]{1,0:T(8,128)(2,1)} %param.10), kind=kOutput, calls=%fused_computation.35 | convolution fusion | flops 4294967296 | bytes 14680064 | tf_op jit(solution)/shard_map/dot_general | solution.py:63
  61.8 2.4 %pad_maximum_fusion = f32[512,2176]{1,0:T(8,128)} fusion(f32[512,128]{1,0:T(8,128)S(1)} %fusion.2, f32[512,2048]{1,0:T(8,128)S(1)} %fusion.25), kind=kLoop, calls=%fused_computation | loop fusion | flops 1114112 | bytes 8912896 | tf_op jit(solution)/shard_map/concatenate | solution.py:66
  64.2 0.0 reduce-scatter.7.cloned.1.call-update
  64.2 0.0 reduce-scatter.11.cloned.1.call-start
  64.2 51.0 %reduce-scatter.7.cloned.1.call-done = f32[128,2176]{1,0:T(8,128)} async-done(((f32[512,2176]{1,0:T(8,128)}), f32[128,2176]{1,0:T(8,128)}) %reduce-scatter.7.cloned.1.call-update) | async-done | bytes 1114128 | tf_op jit(solution)/shard_map/reduce_scatter | solution.py:65
  115.3 1.2 fusion.8
  116.4 0.3 concatenate.22
  116.8 1.4 fusion.4
  118.2 0.3 concatenate.23
  118.5 0.3 fusion.1
  118.9 0.0 copy-start.5
  118.9 0.1 copy.20
  119.0 1.2 reshape.45
  120.1 0.0 reduce-scatter.11.cloned.1.call-update
  120.2 1.2 fusion.10
  121.3 1.2 fusion.6
  122.5 0.1 copy.19
  122.6 0.7 stack.2
  123.3 3.3 %all-to-all-start.1 = ((bf16[4,128,128]{2,1,0:T(8,128)(2,1)}), bf16[4,128,128]{2,1,0:T(8,128)(2,1)S(1)}, u32[]{:S(2)}, u32[]{:S(2)}) async-start(bf16[4,128,128]{2,1,0:T(8,128)(2,1)} %stack.2), calls=%async_computation.2 | async-start | bytes 262144 | tf_op jit(solution)/shard_map/all_to_all | solution.py:57
  126.6 0.0 reduce-scatter.13.cloned.1.call-start
  126.7 15.0 %reduce-scatter.11.cloned.1.call-done = f32[64,512]{1,0:T(8,128)} async-done(((f32[64,2048]{1,0:T(8,128)}), f32[64,512]{1,0:T(8,128)}) %reduce-scatter.11.cloned.1.call-update) | async-done | bytes 131088 | tf_op jit(solution)/shard_map/reduce_scatter | solution.py:95
  141.7 1.7 copy.22
  143.4 0.0 reduce-scatter.13.cloned.1.call-update
  143.5 0.0 reduce-scatter.9.cloned.1.call-start
  143.5 0.0 all-to-all-done.1
  143.5 3.1 %fusion.26 = f32[128,2048]{1,0:T(8,128)} fusion(bf16[512,128]{1,0:T(8,128)(2,1)S(1)} %bitcast.31, bf16[512,2048]{1,0:T(8,128)(2,1)} %bitcast.28), kind=kOutput, calls=%fused_computation.36 | convolution fusion | flops 268435456 | bytes 3276800 | tf_op jit(solution)/shard_map/dot_general | solution.py:59
  146.7 0.0 reduce-scatter.9.cloned.1.call-update
  146.7 0.0 copy-done.2
  146.7 1.3 fusion.13
  148.0 1.3 fusion.16
  149.3 1.1 fusion
  150.4 31.9 %reduce-scatter.13.cloned.1.call-done = f32[64,64]{1,0:T(8,128)} async-done(((f32[512,64]{1,0:T(8,128)}), f32[64,64]{1,0:T(8,128)}) %reduce-scatter.13.cloned.1.call-update) | async-done | bytes 16400
  182.3 1.5 copy.23
  183.7 39.1 %reduce-scatter.9.cloned.1.call-done = f32[16,2048]{1,0:T(8,128)} async-done(((f32[128,2048]{1,0:T(8,128)}), f32[16,2048]{1,0:T(8,128)}) %reduce-scatter.9.cloned.1.call-update) | async-done | bytes 131088 | tf_op jit(solution)/shard_map/reduce_scatter | solution.py:79
  (9 shorter events, 0.0 us)
Async XLA Ops:
  7.2 1.6 copy-start
  7.2 108.1 %reduce-scatter.7.cloned.1.call-start = ((), (), s32[]{:S(2)}) async-start(), calls=%async_computation.6 | async-start | bytes 5570560 | tf_op jit(solution)/shard_map/reduce_scatter | solution.py:65
  8.8 0.8 copy-start.6
  18.7 34.8 %copy-start.4 = (bf16[1,2048,128]{2,1,0:T(8,128)(2,1)S(1)}, bf16[1,2048,128]{2,1,0:T(8,128)(2,1)}, u32[]{:S(2)}) copy-start(bf16[1,2048,128]{2,1,0:T(8,128)(2,1)} %param.11) | copy-start | bytes 1572868
  53.6 1.3 copy-start.1
  64.2 51.1 %copy-start.3 = (bf16[1,128,2048]{2,1,0:T(8,128)(2,1)S(1)}, bf16[1,128,2048]{2,1,0:T(8,128)(2,1)}, u32[]{:S(2)}) copy-start(bf16[1,128,2048]{2,1,0:T(8,128)(2,1)} %param.13) | copy-start | bytes 1572868
  64.2 77.5 %reduce-scatter.11.cloned.1.call-start = ((), (), s32[]{:S(2)}) async-start(), calls=%async_computation.8 | async-start | bytes 655360 | tf_op jit(solution)/shard_map/reduce_scatter | solution.py:95
  118.9 1.3 copy-start.5
  123.3 20.2 %all-to-all-start.1 = ((bf16[4,128,128]{2,1,0:T(8,128)(2,1)}), bf16[4,128,128]{2,1,0:T(8,128)(2,1)S(1)}, u32[]{:S(2)}, u32[]{:S(2)}) async-start(bf16[4,128,128]{2,1,0:T(8,128)(2,1)} %stack.2), calls=%async_computation.2 | async-start | bytes 262144 | tf_op jit(solution)/shard_map/all_to_all | solution.py:57
  126.6 55.7 %reduce-scatter.13.cloned.1.call-start = ((), (), s32[]{:S(2)}) async-start(), calls=%async_computation.9 | async-start | bytes 294912
  143.5 79.4 %reduce-scatter.9.cloned.1.call-start = ((), (), s32[]{:S(2)}) async-start(), calls=%async_computation.7 | async-start | bytes 1179648 | tf_op jit(solution)/shard_map/reduce_scatter | solution.py:79
  143.5 3.2 %copy-start.2 = (f32[128,2176]{1,0:T(8,128)S(1)}, f32[128,2176]{1,0:T(8,128)}, u32[]{:S(2)}) copy-start(f32[128,2176]{1,0:T(8,128)} %reduce-scatter.7.cloned.1.call-done) | copy-start | bytes 3342340
Sparse Core Ops, SparseCore 0:
  64.3 50.9 reduce-scatter.6
  120.3 21.3 reduce-scatter.10
  144.2 38.0 reduce-scatter.12
  185.4 37.4 reduce-scatter.8
